TPU v7x, 32 devices: a whole 2x2x4 slice. The times are simulated.
32 devices in a mesh: gx: 4 (over z), gy: 8 (over y, x, core).
Axes of the slice: x: 2, y: 2, z: 4, core: 2. Of those that a mesh axis runs over, the one named last changes fastest.
Arguments:
- right_side: float32 [512, 2048], P('gx', 'gy'), may hold values from -1.2 to 1.2
- shift: float32 [512, 2048], P('gx', 'gy'), may hold values from 0.0001 to 0.004
Outputs:
- solution: float32 [512, 2048], P('gx', 'gy')
- residual: float32 [512, 2048], P('gx', 'gy')
All inputs are finite; a program needn't handle non-finite values.
Results may differ from a plain program's by a relative error of at most 0.0003.
Values sent between devices are 32-bit elements; how exact they have to be, the bound alone decides.
A program may use at most 128 MiB of HBM per device.

v0:
```python
import jax
import jax.numpy as jnp
from jax import lax
from jax.sharding import PartitionSpec as P

LEVELS = 4
COARSE_SWEEPS = 6
damping = 0.8


def padded_2(cells, sides, width):
    for axis, dim in sides:
        count = lax.axis_size(axis)
        ends = count - 1
        head = lax.slice_in_dim(cells, 0, width, axis=dim)
        tail = lax.slice_in_dim(cells, cells.shape[dim] - width, cells.shape[dim], axis=dim)
        cells = jnp.concatenate(
            [
                lax.ppermute(tail, axis, [(i, (i + 1) % count) for i in range(ends)]),
                cells,
                lax.ppermute(head, axis, [((i + 1) % count, i) for i in range(ends)]),
            ],
            axis=dim,
        )
    return cells


def restrict(values):
    rows, columns = values.shape
    blocks = values.reshape(rows // 2, 2, columns // 2, 2)
    return 0.25 * (
        blocks[:, 0, :, 0] + blocks[:, 1, :, 0] + blocks[:, 0, :, 1] + blocks[:, 1, :, 1]
    )


def prolong(values):
    rows, columns = values.shape
    copies = jnp.broadcast_to(values[:, None, :, None], (rows, 2, columns, 2))
    return copies.reshape(2 * rows, 2 * columns)


def operate_padded(padded, shifts, level):
    centre = padded[1:-1, 1:-1]
    beside = padded[2:, 1:-1] + padded[:-2, 1:-1] + padded[1:-1, 2:] + padded[1:-1, :-2]
    return 4.0 ** (-level) * (4.0 * centre - beside) + shifts * centre


def with_rim(field):
    return padded_2(field, (("gx", 0), ("gy", 1)), 1)


def build_levels(shift):
    levels = []
    shifts = shift
    for level in range(LEVELS + 1):
        diagonal = 4.0 ** (1 - level) + shifts
        outer_shift = None
        inside = None
        levels.append((shifts, diagonal, outer_shift, inside))
        if level < LEVELS:
            shifts = restrict(shifts)
    return levels


def sweep_once(iterate, source, section, level):
    shifts, diagonal = (section[0], section[1])
    if iterate is None:
        return damping * source / diagonal
    return (
        iterate + damping * (source - operate_padded(with_rim(iterate), shifts, level)) / diagonal
    )


def smooth_two(iterate, source, section, level):
    iterate = sweep_once(iterate, source, section, level)
    return sweep_once(iterate, source, section, level)


def residual_of(iterate, source, section, level):
    return source - operate_padded(with_rim(iterate), section[0], level)


def gather_early(field):
    row_band = lax.all_gather(field, "gy", axis=1, tiled=True)
    return lax.all_gather(row_band, "gx", axis=0, tiled=True)


def local_sweeps(iterate, source, shifts, level, count):
    diagonal = 4.0 ** (1 - level) + shifts
    for turn in range(count):
        if iterate is None:
            iterate = damping * source / diagonal
        else:
            iterate = (
                iterate
                + damping * (source - operate_padded(jnp.pad(iterate, 1), shifts, level)) / diagonal
            )
    return iterate


def local_coarse(iterate, source, shifts):
    unit_total = jnp.sum(operate_padded(jnp.pad(jnp.ones_like(source), 1), shifts, LEVELS))
    if iterate is None:
        left = jnp.sum(source)
        iterate = jnp.zeros_like(source) + left / unit_total
    else:
        left = jnp.sum(source - operate_padded(jnp.pad(iterate, 1), shifts, LEVELS))
        iterate = iterate + left / unit_total
    return local_sweeps(iterate, source, shifts, LEVELS, COARSE_SWEEPS)


def local_vcycle(level, iterate, source, shift_table):
    shifts = shift_table[level]
    if level == LEVELS:
        return local_coarse(iterate, source, shifts)
    iterate = local_sweeps(iterate, source, shifts, level, 2)
    coarse_rhs = restrict(source - operate_padded(jnp.pad(iterate, 1), shifts, level))
    iterate = iterate + prolong(local_vcycle(level + 1, None, coarse_rhs, shift_table))
    return local_sweeps(iterate, source, shifts, level, 2)


def local_fcycle(level, source, shift_table):
    shifts = shift_table[level]
    if level == LEVELS:
        return local_coarse(None, source, shifts)
    iterate = local_sweeps(None, source, shifts, level, 2)
    coarse_rhs = restrict(source - operate_padded(jnp.pad(iterate, 1), shifts, level))
    correction = local_fcycle(level + 1, coarse_rhs, shift_table)
    correction = local_vcycle(level + 1, correction, coarse_rhs, shift_table)
    iterate = iterate + prolong(correction)
    return local_sweeps(iterate, source, shifts, level, 2)


def own_block(whole, rows, columns):
    return lax.dynamic_slice(
        whole, (lax.axis_index("gx") * rows, lax.axis_index("gy") * columns), (rows, columns)
    )


def early_solve(coarse_rhs, shift_table, full):
    whole_rhs = gather_early(coarse_rhs)
    if full:
        whole = local_fcycle(LEVELS - 1, whole_rhs, shift_table)
        whole = local_vcycle(LEVELS - 1, whole, whole_rhs, shift_table)
    else:
        whole = local_vcycle(LEVELS - 1, None, whole_rhs, shift_table)
    return own_block(whole, coarse_rhs.shape[0], coarse_rhs.shape[1])


def vcycle(level, iterate, source, levels, shift_whole):
    section = levels[level]
    iterate = smooth_two(iterate, source, section, level)
    coarse_rhs = restrict(residual_of(iterate, source, section, level))
    if level + 1 == LEVELS - 1:
        correction = early_solve(coarse_rhs, shift_whole, False)
    else:
        correction = vcycle(level + 1, None, coarse_rhs, levels, shift_whole)
    iterate = iterate + prolong(correction)
    return smooth_two(iterate, source, section, level)


def fcycle(level, source, levels, shift_whole):
    section = levels[level]
    iterate = smooth_two(None, source, section, level)
    coarse_rhs = restrict(residual_of(iterate, source, section, level))
    if level + 1 == LEVELS - 1:
        correction = early_solve(coarse_rhs, shift_whole, True)
    else:
        correction = fcycle(level + 1, coarse_rhs, levels, shift_whole)
        correction = vcycle(level + 1, correction, coarse_rhs, levels, shift_whole)
    iterate = iterate + prolong(correction)
    return smooth_two(iterate, source, section, level)


def body(right_side, shift):
    levels = build_levels(shift)
    upper = gather_early(levels[LEVELS - 1][0])
    shift_whole = {LEVELS - 1: upper, LEVELS: restrict(upper)}
    solution = fcycle(0, right_side, levels, shift_whole)
    residual = residual_of(solution, right_side, levels[0], 0)
    return (solution, residual)


def solution(mesh):
    in_specs = (P("gx", "gy"), P("gx", "gy"))
    out_specs = (P("gx", "gy"), P("gx", "gy"))
    return jax.shard_map(body, mesh=mesh, in_specs=in_specs, out_specs=out_specs, check_vma=False)
```

profile of v0, /device:TPU:28, one launch (start us, length us, event | category | flops | bytes accessed | tf_op | source)
XLA Modules:
  0.0 715.0 jit_solution(5198619085677997498)
XLA Ops:
  5.3 10.5 %reshape.185 = f32[64,2,128,2]{3,2,1,0:T(8,128)} reshape(f32[128,256]{1,0:T(8,128)} %param.3) | data formatting | bytes 262144 | tf_op jit(solution)/shard_map/reshape | solution.py:30
  20.4 8.0 %fusion.1 = f32[64,128]{1,0:T(8,128)S(1)} fusion(f32[64,2,128,2]{3,2,1,0:T(8,128)} %reshape.185), kind=kLoop, calls=%fused_computation.2 | loop fusion | flops 32768 | bytes 163840 | tf_op jit(solution)/shard_map/mul | solution.py:31
  30.7 4.5 collective-permute-start.4
  46.0 4.4 collective-permute-done.7
  50.5 9.8 %reshape.184 = f32[64,2,128,2]{3,2,1,0:T(8,128)} reshape(f32[128,256]{1,0:T(8,128)S(1)} %fusion.39) | data formatting | bytes 262144 | tf_op jit(solution)/shard_map/reshape | solution.py:30
  60.3 8.5 %multiply_reduce_fusion = (f32[64,128]{1,0:T(8,128)S(1)}, f32[64,128]{1,0:T(8,128)S(1)}) fusion(f32[64,2,128,2]{3,2,1,0:T(8,128)} %reshape.184), kind=kLoop, calls=%fused_computation.8 | loop fusion | flops 40960 | bytes 196608 | tf_op jit(solution)/shard_map/mul | solution.py:31
  72.8 14.8 %all-gather.2 = f32[16,1,256,1]{3,2,1,0:T(8,128)S(1)} all-gather(f32[16,1,32,1]{3,2,1,0:T(8,128)S(1)} %fusion.10), channel_id=4, replica_groups=mesh['gx'=4,'gy'=8] {'gy'}, dimensions={2}, use_global_device_ids=true | all-gather | bytes 18432 | tf_op jit(solution)/shard_map/all_gather | solution.py:84
  93.7 13.6 %all-gather.3 = f32[64,1,256,1]{2,3,1,0:T(1,128)S(1)} all-gather(f32[16,1,256,1]{2,3,1,0:T(1,128)S(1)} %copy.135), channel_id=5, replica_groups=mesh['gx'=4,'gy'=8] {'gx'}, dimensions={0}, use_global_device_ids=true | all-gather | bytes 81920 | tf_op jit(solution)/shard_map/all_gather | solution.py:85
  111.4 5.6 reshape.189
  128.6 4.5 collective-permute-start.16
  163.9 14.8 %all-gather = f32[16,1,256,1]{3,2,1,0:T(8,128)S(1)} all-gather(f32[16,1,32,1]{3,2,1,0:T(8,128)S(1)} %fusion.11), channel_id=2, replica_groups=mesh['gx'=4,'gy'=8] {'gy'}, dimensions={2}, use_global_device_ids=true | all-gather | bytes 18432 | tf_op jit(solution)/shard_map/all_gather | solution.py:84
  179.3 13.1 %all-gather.1 = f32[64,1,256,1]{2,3,1,0:T(1,128)S(1)} all-gather(f32[16,1,256,1]{2,3,1,0:T(1,128)S(1)} %copy.134), channel_id=3, replica_groups=mesh['gx'=4,'gy'=8] {'gx'}, dimensions={0}, use_global_device_ids=true | all-gather | bytes 81920 | tf_op jit(solution)/shard_map/all_gather | solution.py:85
  192.7 5.6 reshape.188
  198.3 8.6 %multiply_reduce_fusion.6 = (f32[32,128]{1,0:T(8,128)S(1)}, f32[32,1,128,1]{3,2,1,0:T(8,128)S(1)}, f32[]{:T(128)}, f32[32,128]{1,0:T(8,128)S(1)}) fusion(f32[32,2,128,2]{3,2,1,0:T(8,128)} %reshape.189, f32[32,2,128,2]{3,2,1,0:T(8,128)} %reshape.188), kind=kLoop, calls=%fused_computation.33 | loop fusion | flops 36863 | bytes 180228 | tf_op jit(solution)/shard_map/mul | solution.py:31
  220.0 5.6 reshape.191
  225.6 5.8 fusion.727
  241.3 10.9 %collective-permute-start.24 = (f32[1,64]{1,0:T(1,128)S(1)}, f32[1,64]{1,0:T(1,128)S(1)}, u32[]{:S(2)}, u32[]{:S(2)}) collective-permute-start(f32[1,64]{1,0:T(1,128)S(1)} %get-tuple-element.123), channel_id=1, source_target_pairs={{8,0},{16,8},{24,16},{9,1},{17,9},{25,17},{10,2},{18,10},{26,18},{... | collective-permute-start | bytes 776 | tf_op jit(solution)/shard_map/ppermute | solution.py:21
  269.9 4.2 collective-permute-done.29
  331.4 15.1 %all-gather.4 = f32[16,1,256,1]{3,2,1,0:T(8,128)} all-gather(f32[16,1,32,1]{3,2,1,0:T(8,128)S(1)} %fusion.9), channel_id=6, replica_groups=mesh['gx'=4,'gy'=8] {'gy'}, dimensions={2}, use_global_device_ids=true | all-gather | bytes 18432 | tf_op jit(solution)/shard_map/all_gather | solution.py:84
  348.7 13.1 %all-gather.5 = f32[64,1,256,1]{2,3,1,0:T(1,128)S(1)} all-gather(f32[16,1,256,1]{2,3,1,0:T(1,128)S(1)} %copy.136), channel_id=7, replica_groups=mesh['gx'=4,'gy'=8] {'gx'}, dimensions={0}, use_global_device_ids=true | all-gather | bytes 81920 | tf_op jit(solution)/shard_map/all_gather | solution.py:85
  362.1 5.6 reshape.195
  367.7 5.8 fusion.726
  537.2 15.1 %all-gather.6 = f32[16,1,256,1]{3,2,1,0:T(8,128)} all-gather(f32[16,1,32,1]{3,2,1,0:T(8,128)S(1)} %fusion.8), channel_id=8, replica_groups=mesh['gx'=4,'gy'=8] {'gy'}, dimensions={2}, use_global_device_ids=true | all-gather | bytes 18432 | tf_op jit(solution)/shard_map/all_gather | solution.py:84
  554.5 13.1 %all-gather.7 = f32[64,1,256,1]{2,3,1,0:T(1,128)S(1)} all-gather(f32[16,1,256,1]{2,3,1,0:T(1,128)S(1)} %copy.137), channel_id=9, replica_groups=mesh['gx'=4,'gy'=8] {'gx'}, dimensions={0}, use_global_device_ids=true | all-gather | bytes 81920 | tf_op jit(solution)/shard_map/all_gather | solution.py:85
  567.9 5.6 reshape.201
  573.4 5.8 fusion.725
  591.8 4.2 collective-permute-done.81
  626.3 4.2 collective-permute-done.89
  658.5 6.9 reshape.205
  668.7 4.2 collective-permute-done.97
  684.8 4.2 collective-permute-done.101
  701.0 4.2 collective-permute-done.105
  (441 shorter events, 445.1 us)
Async XLA Ops:
  1.6 14.2 %collective-permute-start = (f32[1,256]{1,0:T(1,128)S(1)}, f32[1,256]{1,0:T(1,128)S(1)}, u32[]{:S(2)}, u32[]{:S(2)}) collective-permute-start(f32[1,256]{1,0:T(1,128)S(1)} %get-tuple-element.37), channel_id=1, source_target_pairs={{8,0},{16,8},{24,16},{9,1},{17,9},{25,17},{10,2},{18,10},{26,18},{... | collective-permute-start | bytes 3080 | tf_op jit(solution)/shard_map/ppermute | solution.py:21
  4.0 11.8 %collective-permute-start.1 = (f32[1,256]{1,0:T(1,128)S(1)}, f32[1,256]{1,0:T(1,128)S(1)}, u32[]{:S(2)}, u32[]{:S(2)}) collective-permute-start(f32[1,256]{1,0:T(1,128)S(1)} %get-tuple-element.36), channel_id=1, source_target_pairs={{0,8},{8,16},{16,24},{1,9},{9,17},{17,25},{2,10},{10,18},{18,26},{... | collective-permute-start | bytes 3080 | tf_op jit(solution)/shard_map/ppermute | solution.py:19
  16.0 14.6 %collective-permute-start.2 = (f32[130,1]{1,0:T(8,128)S(1)}, f32[130,1]{1,0:T(8,128)S(1)}, u32[]{:S(2)}, u32[]{:S(2)}) collective-permute-start(f32[130,1]{1,0:T(8,128)S(1)} %get-tuple-element.26), channel_id=1, source_target_pairs={{1,0},{2,1},{3,2},{4,3},{5,4},{6,5},{7,6},{9,8},{10,9},{11,10},{12... | collective-permute-start | bytes 1568 | tf_op jit(solution)/shard_map/ppermute | solution.py:21
  18.5 12.1 %collective-permute-start.3 = (f32[130,1]{1,0:T(8,128)S(1)}, f32[130,1]{1,0:T(8,128)S(1)}, u32[]{:S(2)}, u32[]{:S(2)}) collective-permute-start(f32[130,1]{1,0:T(8,128)S(1)} %get-tuple-element.27), channel_id=1, source_target_pairs={{0,1},{1,2},{2,3},{3,4},{4,5},{5,6},{6,7},{8,9},{9,10},{10,11},{11... | collective-permute-start | bytes 1568 | tf_op jit(solution)/shard_map/ppermute | solution.py:19
  30.7 7.2 %collective-permute-start.4 = (f32[1,256]{1,0:T(1,128)S(1)}, f32[1,256]{1,0:T(1,128)S(1)}, u32[]{:S(2)}, u32[]{:S(2)}) collective-permute-start(f32[1,256]{1,0:T(1,128)S(1)} %get-tuple-element.35), channel_id=1, source_target_pairs={{8,0},{16,8},{24,16},{9,1},{17,9},{25,17},{10,2},{18,10},{26,18},{... | collective-permute-start | bytes 3080 | tf_op jit(solution)/shard_map/ppermute | solution.py:21
  43.8 6.5 collective-permute-start.7
  68.9 19.4 %collective-permute-start.8 = (f32[1,128]{1,0:T(1,128)S(1)}, f32[1,128]{1,0:T(1,128)S(1)}, u32[]{:S(2)}, u32[]{:S(2)}) collective-permute-start(f32[1,128]{1,0:T(1,128)S(1)} %get-tuple-element.75), channel_id=1, source_target_pairs={{8,0},{16,8},{24,16},{9,1},{17,9},{25,17},{10,2},{18,10},{26,18},{... | collective-permute-start | bytes 1544 | tf_op jit(solution)/shard_map/ppermute | solution.py:21
  71.5 16.8 %collective-permute-start.9 = (f32[1,128]{1,0:T(1,128)S(1)}, f32[1,128]{1,0:T(1,128)S(1)}, u32[]{:S(2)}, u32[]{:S(2)}) collective-permute-start(f32[1,128]{1,0:T(1,128)S(1)} %get-tuple-element.74), channel_id=1, source_target_pairs={{0,8},{8,16},{16,24},{1,9},{9,17},{17,25},{2,10},{10,18},{18,26},{... | collective-permute-start | bytes 1544 | tf_op jit(solution)/shard_map/ppermute | solution.py:19
  88.4 18.9 %collective-permute-start.10 = (f32[66,1]{1,0:T(8,128)S(1)}, f32[66,1]{1,0:T(8,128)S(1)}, u32[]{:S(2)}, u32[]{:S(2)}) collective-permute-start(f32[66,1]{1,0:T(8,128)S(1)} %get-tuple-element.56), channel_id=1, source_target_pairs={{1,0},{2,1},{3,2},{4,3},{5,4},{6,5},{7,6},{9,8},{10,9},{11,10},{12... | collective-permute-start | bytes 800 | tf_op jit(solution)/shard_map/ppermute | solution.py:21
  91.7 15.5 %collective-permute-start.11 = (f32[66,1]{1,0:T(8,128)S(1)}, f32[66,1]{1,0:T(8,128)S(1)}, u32[]{:S(2)}, u32[]{:S(2)}) collective-permute-start(f32[66,1]{1,0:T(8,128)S(1)} %get-tuple-element.57), channel_id=1, source_target_pairs={{0,1},{1,2},{2,3},{3,4},{4,5},{5,6},{6,7},{8,9},{9,10},{10,11},{11... | collective-permute-start | bytes 800 | tf_op jit(solution)/shard_map/ppermute | solution.py:19
  107.4 9.6 %collective-permute-start.12 = (f32[1,128]{1,0:T(1,128)S(1)}, f32[1,128]{1,0:T(1,128)S(1)}, u32[]{:S(2)}, u32[]{:S(2)}) collective-permute-start(f32[1,128]{1,0:T(1,128)S(1)} %get-tuple-element.73), channel_id=1, source_target_pairs={{8,0},{16,8},{24,16},{9,1},{17,9},{25,17},{10,2},{18,10},{26,18},{... | collective-permute-start | bytes 1544 | tf_op jit(solution)/shard_map/ppermute | solution.py:21
  110.0 7.0 collective-permute-start.13
  119.0 6.2 collective-permute-start.15
  140.6 6.0 collective-permute-start.19
  157.0 6.0 collective-permute-start.23
  241.3 12.2 %collective-permute-start.24 = (f32[1,64]{1,0:T(1,128)S(1)}, f32[1,64]{1,0:T(1,128)S(1)}, u32[]{:S(2)}, u32[]{:S(2)}) collective-permute-start(f32[1,64]{1,0:T(1,128)S(1)} %get-tuple-element.123), channel_id=1, source_target_pairs={{8,0},{16,8},{24,16},{9,1},{17,9},{25,17},{10,2},{18,10},{26,18},{... | collective-permute-start | bytes 776 | tf_op jit(solution)/shard_map/ppermute | solution.py:21
  259.7 6.0 collective-permute-start.27
  276.0 6.0 collective-permute-start.31
  293.5 6.0 collective-permute-start.35
  309.1 6.0 collective-permute-start.39
  429.3 6.2 collective-permute-start.55
  445.0 6.2 collective-permute-start.59
  460.9 6.2 collective-permute-start.63
  476.7 6.2 collective-permute-start.67
  492.4 6.2 collective-permute-start.71
  514.8 6.0 collective-permute-start.75
  615.4 6.0 collective-permute-start.87
  632.5 6.2 collective-permute-start.91
  648.2 6.2 collective-permute-start.95
  674.9 6.5 collective-permute-start.99
  691.0 6.5 collective-permute-start.103
  707.2 6.5 collective-permute-start.107
  (79 other events, 371.7 us)
where the time goes:
time: 727 us; the launch traced here: 715 us
  starting transfers between devices  227 us (31%)
  waiting for transfers between devices  192 us (26%)
  blocking collectives  113 us (16%)
  local copies, waits for them, and re-layouts  110 us (15%)
  other arithmetic  62.6 us (9%)
  between operations  10.1 us (1%)
    ppermute x54, waiting for transfers between devices, padded_2(): lax.ppermute(tail, axis, [(i, (i + 1) % count) for i in range(ends)])  191 us
    ppermute x54, starting transfers between devices, padded_2(): lax.ppermute(head, axis, [((i + 1) % count, i) for i in range(ends)])  129 us
    ppermute x54, starting transfers between devices, padded_2(): lax.ppermute(tail, axis, [(i, (i + 1) % count) for i in range(ends)])  98.4 us
    all_gather x4, blocking collectives, gather_early(): row_band = lax.all_gather(field, 'gy', axis=1, tiled=True)  59.9 us
    reshape x12, local copies, waits for them, and re-layouts, restrict(): blocks = values.reshape(rows // 2, 2, columns // 2, 2)  55.2 us
    all_gather x4, blocking collectives, gather_early(): return lax.all_gather(row_band, 'gx', axis=0, tiled=True)  53 us
    mul x13, other arithmetic, restrict(): 0.25 * (blocks[:, 0, :, 0] + blocks[:, 1, :, 0] + blocks[:, 0, :, 1] + bl...  48.9 us
    reshape x10, local copies, waits for them, and re-layouts, prolong(): return copies.reshape(2 * rows, 2 * columns)  27.8 us
  transfers between devices with their start and end apart: 108, of which 49 were waited for; matrix products, arithmetic and copies ran while one was open for 4% of the time, Pallas kernels for 0%

commit v1 on v0

--- a/solution.py
+++ b/solution.py
@@ -81,7 +81,7 @@
 
 
 def gather_early(field):
-    row_band = lax.all_gather(field, "gy", axis=1, tiled=True)
+    row_band = jnp.concatenate(lax.all_gather(field, "gy"), axis=1)
     return lax.all_gather(row_band, "gx", axis=0, tiled=True)
 
 

time: 727 us -> 697 us (0.959)
  blocking collectives: 113 us -> 84.9 us
  starting transfers between devices: 227 us -> 216 us
    all_gather x4, blocking collectives: 59.9 us -> 32.2 us  [gather_early(): row_band = jnp.concatenate(lax.all_gather(field, 'gy'), axis=1)]
    ppermute x54, starting transfers between devices: 129 us -> 116 us  [padded_2(): lax.ppermute(head, axis, [((i + 1) % count, i) for i in range(ends)])]
    unnamed x10 -> x32, local copies, waits for them, and re-layouts: 0.04 us -> 8.38 us
  transfers between devices with their start and end apart: 108 -> 108, of which waited for: 49 -> 50; matrix products, arithmetic and copies ran while one was open for 4% -> 4% of each run, Pallas kernels for 0% -> 0%
where the time goes in v1:
time: 697 us; the launch traced here: 685 us
  starting transfers between devices  216 us (31%)
  waiting for transfers between devices  195 us (28%)
  local copies, waits for them, and re-layouts  116 us (17%)
  blocking collectives  84.9 us (12%)
  other arithmetic  63.1 us (9%)
  between operations  9.8 us (1%)
    ppermute x54, waiting for transfers between devices, padded_2(): lax.ppermute(tail, axis, [(i, (i + 1) % count) for i in range(ends)])  195 us
    ppermute x54, starting transfers between devices, padded_2(): lax.ppermute(head, axis, [((i + 1) % count, i) for i in range(ends)])  116 us
    ppermute x54, starting transfers between devices, padded_2(): lax.ppermute(tail, axis, [(i, (i + 1) % count) for i in range(ends)])  99.7 us
    reshape x12, local copies, waits for them, and re-layouts, restrict(): blocks = values.reshape(rows // 2, 2, columns // 2, 2)  55.2 us
    all_gather x4, blocking collectives, gather_early(): return lax.all_gather(row_band, 'gx', axis=0, tiled=True)  52.7 us
    mul x13, other arithmetic, restrict(): 0.25 * (blocks[:, 0, :, 0] + blocks[:, 1, :, 0] + blocks[:, 0, :, 1] + bl...  48.1 us
    all_gather x4, blocking collectives, gather_early(): row_band = jnp.concatenate(lax.all_gather(field, 'gy'), axis=1)  32.2 us
    reshape x10, local copies, waits for them, and re-layouts, prolong(): return copies.reshape(2 * rows, 2 * columns)  27.8 us
  transfers between devices with their start and end apart: 108, of which 50 were waited for; matrix products, arithmetic and copies ran while one was open for 4% of the time, Pallas kernels for 0%

profile of v1, /device:TPU:28, one launch (start us, length us, event | category | flops | bytes accessed | tf_op | source)
XLA Modules:
  0.0 684.8 jit_solution(17025281811054120344)
XLA Ops:
  5.3 10.5 %reshape.369 = f32[64,2,128,2]{3,2,1,0:T(8,128)} reshape(f32[128,256]{1,0:T(8,128)} %param.3) | data formatting | bytes 262144 | tf_op jit(solution)/shard_map/reshape | solution.py:30
  20.4 8.0 %fusion.1 = f32[64,128]{1,0:T(8,128)S(1)} fusion(f32[64,2,128,2]{3,2,1,0:T(8,128)} %reshape.369), kind=kLoop, calls=%fused_computation.2 | loop fusion | flops 32768 | bytes 163840 | tf_op jit(solution)/shard_map/mul | solution.py:31
  30.7 4.5 collective-permute-start.4
  50.5 9.8 %reshape.368 = f32[64,2,128,2]{3,2,1,0:T(8,128)} reshape(f32[128,256]{1,0:T(8,128)S(1)} %fusion.35) | data formatting | bytes 262144 | tf_op jit(solution)/shard_map/reshape | solution.py:30
  60.3 8.5 %multiply_reduce_fusion = (f32[64,128]{1,0:T(8,128)S(1)}, f32[64,128]{1,0:T(8,128)S(1)}) fusion(f32[64,2,128,2]{3,2,1,0:T(8,128)} %reshape.368), kind=kLoop, calls=%fused_computation.8 | loop fusion | flops 40960 | bytes 196608 | tf_op jit(solution)/shard_map/mul | solution.py:31
  81.4 8.8 %all-gather.1 = f32[128,1,32,1]{2,3,1,0:T(1,128)S(1)} all-gather(f32[16,1,32,1]{2,3,1,0:T(1,128)S(1)} %bitcast.40), channel_id=3, replica_groups=mesh['gx'=4,'gy'=8] {'gy'}, dimensions={0}, use_global_device_ids=true | all-gather | bytes 18432 | tf_op jit(solution)/shard_map/all_gather | solution.py:84
  94.4 13.3 %all_gather.31 = f32[64,256]{1,0:T(8,128)S(1)} all-gather(f32[16,256]{1,0:T(8,128)S(1)} %reshape.375), channel_id=1, replica_groups=mesh['gx'=4,'gy'=8] {'gx'}, dimensions={0}, use_global_device_ids=true | all-gather | bytes 81920 | tf_op jit(solution)/shard_map/all_gather | solution.py:85
  107.7 5.5 reshape.377
  128.8 4.2 collective-permute-done.17
  145.2 4.2 collective-permute-done.21
  158.9 7.8 %all-gather = f32[128,1,32,1]{2,3,1,0:T(1,128)S(1)} all-gather(f32[16,1,32,1]{2,3,1,0:T(1,128)S(1)} %bitcast.41), channel_id=2, replica_groups=mesh['gx'=4,'gy'=8] {'gy'}, dimensions={0}, use_global_device_ids=true | all-gather | bytes 18432 | tf_op jit(solution)/shard_map/all_gather | solution.py:84
  166.8 13.1 %all_gather.29 = f32[64,256]{1,0:T(8,128)S(1)} all-gather(f32[16,256]{1,0:T(8,128)S(1)} %reshape.373), channel_id=1, replica_groups=mesh['gx'=4,'gy'=8] {'gx'}, dimensions={0}, use_global_device_ids=true | all-gather | bytes 81920 | tf_op jit(solution)/shard_map/all_gather | solution.py:85
  180.2 5.6 reshape.376
  185.8 8.6 %multiply_reduce_fusion.6 = (f32[32,128]{1,0:T(8,128)S(1)}, f32[32,1,128,1]{3,2,1,0:T(8,128)S(1)}, f32[]{:T(128)}, f32[32,128]{1,0:T(8,128)S(1)}) fusion(f32[32,2,128,2]{3,2,1,0:T(8,128)} %reshape.377, f32[32,2,128,2]{3,2,1,0:T(8,128)} %reshape.376), kind=kLoop, calls=%fused_computation.33 | loop fusion | flops 36863 | bytes 180228 | tf_op jit(solution)/shard_map/mul | solution.py:31
  207.2 5.6 reshape.379
  212.8 5.8 fusion.723
  232.1 4.2 collective-permute-done.25
  248.5 4.2 collective-permute-done.29
  266.0 4.2 collective-permute-done.33
  314.3 7.8 %all-gather.2 = f32[128,1,32,1]{2,3,1,0:T(1,128)S(1)} all-gather(f32[16,1,32,1]{2,3,1,0:T(1,128)S(1)} %bitcast.42), channel_id=4, replica_groups=mesh['gx'=4,'gy'=8] {'gy'}, dimensions={0}, use_global_device_ids=true | all-gather | bytes 18432 | tf_op jit(solution)/shard_map/all_gather | solution.py:84
  322.3 13.1 %all_gather.33 = f32[64,256]{1,0:T(8,128)S(1)} all-gather(f32[16,256]{1,0:T(8,128)S(1)} %reshape.384), channel_id=1, replica_groups=mesh['gx'=4,'gy'=8] {'gx'}, dimensions={0}, use_global_device_ids=true | all-gather | bytes 81920 | tf_op jit(solution)/shard_map/all_gather | solution.py:85
  335.7 5.6 reshape.385
  341.2 5.9 fusion.722
  460.5 4.2 collective-permute-done.69
  515.9 7.8 %all-gather.3 = f32[128,1,32,1]{2,3,1,0:T(1,128)S(1)} all-gather(f32[16,1,32,1]{2,3,1,0:T(1,128)S(1)} %bitcast.43), channel_id=5, replica_groups=mesh['gx'=4,'gy'=8] {'gy'}, dimensions={0}, use_global_device_ids=true | all-gather | bytes 18432 | tf_op jit(solution)/shard_map/all_gather | solution.py:84
  523.8 13.1 %all_gather.35 = f32[64,256]{1,0:T(8,128)S(1)} all-gather(f32[16,256]{1,0:T(8,128)S(1)} %reshape.392), channel_id=1, replica_groups=mesh['gx'=4,'gy'=8] {'gx'}, dimensions={0}, use_global_device_ids=true | all-gather | bytes 81920 | tf_op jit(solution)/shard_map/all_gather | solution.py:85
  537.2 5.6 reshape.393
  542.8 5.9 fusion.721
  628.4 6.9 %reshape.397 = f32[128,256]{1,0:T(8,128)S(1)} reshape(f32[64,2,128,2]{3,2,1,0:T(8,128)} %broadcast_in_dim.29) | data formatting | bytes 262144 | tf_op jit(solution)/shard_map/reshape | solution.py:39
  638.6 4.2 collective-permute-done.97
  654.7 4.2 collective-permute-done.101
  670.8 4.2 collective-permute-done.105
  (470 shorter events, 450.6 us)
Async XLA Ops:
  1.6 14.2 %collective-permute-start = (f32[1,256]{1,0:T(1,128)S(1)}, f32[1,256]{1,0:T(1,128)S(1)}, u32[]{:S(2)}, u32[]{:S(2)}) collective-permute-start(f32[1,256]{1,0:T(1,128)S(1)} %get-tuple-element.53), channel_id=1, source_target_pairs={{8,0},{16,8},{24,16},{9,1},{17,9},{25,17},{10,2},{18,10},{26,18},{... | collective-permute-start | bytes 3080 | tf_op jit(solution)/shard_map/ppermute | solution.py:21
  4.0 11.8 %collective-permute-start.1 = (f32[1,256]{1,0:T(1,128)S(1)}, f32[1,256]{1,0:T(1,128)S(1)}, u32[]{:S(2)}, u32[]{:S(2)}) collective-permute-start(f32[1,256]{1,0:T(1,128)S(1)} %get-tuple-element.52), channel_id=1, source_target_pairs={{0,8},{8,16},{16,24},{1,9},{9,17},{17,25},{2,10},{10,18},{18,26},{... | collective-permute-start | bytes 3080 | tf_op jit(solution)/shard_map/ppermute | solution.py:19
  15.9 14.5 %collective-permute-start.2 = (f32[130,1]{1,0:T(8,128)S(1)}, f32[130,1]{1,0:T(8,128)S(1)}, u32[]{:S(2)}, u32[]{:S(2)}) collective-permute-start(f32[130,1]{1,0:T(8,128)S(1)} %get-tuple-element.42), channel_id=1, source_target_pairs={{1,0},{2,1},{3,2},{4,3},{5,4},{6,5},{7,6},{9,8},{10,9},{11,10},{12... | collective-permute-start | bytes 1568 | tf_op jit(solution)/shard_map/ppermute | solution.py:21
  18.5 12.0 %collective-permute-start.3 = (f32[130,1]{1,0:T(8,128)S(1)}, f32[130,1]{1,0:T(8,128)S(1)}, u32[]{:S(2)}, u32[]{:S(2)}) collective-permute-start(f32[130,1]{1,0:T(8,128)S(1)} %get-tuple-element.43), channel_id=1, source_target_pairs={{0,1},{1,2},{2,3},{3,4},{4,5},{5,6},{6,7},{8,9},{9,10},{10,11},{11... | collective-permute-start | bytes 1568 | tf_op jit(solution)/shard_map/ppermute | solution.py:19
  30.7 7.2 %collective-permute-start.4 = (f32[1,256]{1,0:T(1,128)S(1)}, f32[1,256]{1,0:T(1,128)S(1)}, u32[]{:S(2)}, u32[]{:S(2)}) collective-permute-start(f32[1,256]{1,0:T(1,128)S(1)} %get-tuple-element.51), channel_id=1, source_target_pairs={{8,0},{16,8},{24,16},{9,1},{17,9},{25,17},{10,2},{18,10},{26,18},{... | collective-permute-start | bytes 3080 | tf_op jit(solution)/shard_map/ppermute | solution.py:21
  43.8 6.5 collective-permute-start.7
  77.0 13.2 %collective-permute-start.10 = (f32[66,1]{1,0:T(8,128)S(1)}, f32[66,1]{1,0:T(8,128)S(1)}, u32[]{:S(2)}, u32[]{:S(2)}) collective-permute-start(f32[66,1]{1,0:T(8,128)S(1)} %get-tuple-element.72), channel_id=1, source_target_pairs={{1,0},{2,1},{3,2},{4,3},{5,4},{6,5},{7,6},{9,8},{10,9},{11,10},{12... | collective-permute-start | bytes 800 | tf_op jit(solution)/shard_map/ppermute | solution.py:21
  78.9 11.3 %collective-permute-start.11 = (f32[66,1]{1,0:T(8,128)S(1)}, f32[66,1]{1,0:T(8,128)S(1)}, u32[]{:S(2)}, u32[]{:S(2)}) collective-permute-start(f32[66,1]{1,0:T(8,128)S(1)} %get-tuple-element.73), channel_id=1, source_target_pairs={{0,1},{1,2},{2,3},{3,4},{4,5},{5,6},{6,7},{8,9},{9,10},{10,11},{11... | collective-permute-start | bytes 800 | tf_op jit(solution)/shard_map/ppermute | solution.py:19
  90.4 22.9 %collective-permute-start.12 = (f32[1,128]{1,0:T(1,128)S(1)}, f32[1,128]{1,0:T(1,128)S(1)}, u32[]{:S(2)}, u32[]{:S(2)}) collective-permute-start(f32[1,128]{1,0:T(1,128)S(1)} %get-tuple-element.89), channel_id=1, source_target_pairs={{8,0},{16,8},{24,16},{9,1},{17,9},{25,17},{10,2},{18,10},{26,18},{... | collective-permute-start | bytes 1544 | tf_op jit(solution)/shard_map/ppermute | solution.py:21
  92.8 20.5 %collective-permute-start.13 = (f32[1,128]{1,0:T(1,128)S(1)}, f32[1,128]{1,0:T(1,128)S(1)}, u32[]{:S(2)}, u32[]{:S(2)}) collective-permute-start(f32[1,128]{1,0:T(1,128)S(1)} %get-tuple-element.88), channel_id=1, source_target_pairs={{0,8},{8,16},{16,24},{1,9},{9,17},{17,25},{2,10},{10,18},{18,26},{... | collective-permute-start | bytes 1544 | tf_op jit(solution)/shard_map/ppermute | solution.py:19
  115.3 6.2 collective-permute-start.15
  135.0 6.0 collective-permute-start.19
  151.3 6.0 collective-permute-start.23
  238.2 6.0 collective-permute-start.27
  254.6 6.0 collective-permute-start.31
  272.1 6.0 collective-permute-start.35
  287.6 6.0 collective-permute-start.39
  303.1 6.0 collective-permute-start.43
  366.5 6.0 collective-permute-start.47
  383.7 6.0 collective-permute-start.51
  403.7 6.2 collective-permute-start.55
  419.4 6.2 collective-permute-start.59
  435.3 6.2 collective-permute-start.63
  451.0 6.2 collective-permute-start.67
  466.7 6.2 collective-permute-start.71
  568.0 6.0 collective-permute-start.83
  585.2 6.0 collective-permute-start.87
  602.4 6.2 collective-permute-start.91
  618.1 6.2 collective-permute-start.95
  644.8 6.5 collective-permute-start.99
  660.9 6.5 collective-permute-start.103
  677.0 6.5 collective-permute-start.107
  (84 other events, 481.6 us)
